TPU v7x, 32 devices: a whole 2x2x4 slice. The times are simulated.
32 devices in a mesh: groups: 2 (over x), depth: 16 (over z, y, core).
Axes of the slice: x: 2, y: 2, z: 4, core: 2. Of those that a mesh axis runs over, the one named last changes fastest.
Arguments:
- fronts: bfloat16 [4, 64, 8, 2048], P(None, ('groups', 'depth')), parts along dimension 1, may hold values from -6 to 6
- extrap: bfloat16 [32, 16, 5, 2, 128, 128], P('depth'), may hold values from -0.15625 to 0.15625
- offsets: int32 [2, 5], replicated, may hold values from -2 to 2
- assign: int32 [2, 8], replicated, may hold values from 0 to 7, each once within a row
Outputs:
- images: float32 [8, 32, 2048], P(None, ('groups', 'depth')), parts along dimension 1
- last_fronts: bfloat16 [4, 64, 8, 2048], P(None, ('groups', 'depth')), parts along dimension 1
There are 2 independent parts, one for each index of `groups`. A program takes and returns all parts, laid end to end along the dimension named above; an argument that names none is the same for every part. Nothing has to cross between parts.
Inputs may be any that keep to these rules, and one draw needn't show every extreme that they name: `assign`: each row names every shot number once.
All inputs are finite; a program needn't handle non-finite values.
Results may differ from a plain program's by a relative error of at most 0.015.
Values may be sent and summed in bfloat16 or wider, within the bound.
A program may use at most 64 MiB of HBM per device.

v0:
```python
import math

import jax
import jax.numpy as jnp
from jax import lax
from jax.sharding import PartitionSpec as P

BLOCK = 128
NBLK = 16
BAND = 5
FOWNERS = 8
HANDOVERS = 8
NFREQ = 16


def from_partner(value, axis, stride):
    mask = 2**stride
    pairs = [(source, source ^ mask) for source in range(lax.axis_size(axis))]
    return lax.ppermute(value, axis, pairs)


def passed_along(shard, axis, by):
    size = lax.axis_size(axis)
    return lax.ppermute(shard, axis, [(i, (i + by) % size) for i in range(size)])


def advance(wave_state, band_offsets, operator):
    reach = BAND // 2
    nfield, freqs, slots, points = wave_state.shape
    blocks = wave_state.reshape(nfield, freqs, slots, NBLK, BLOCK)
    padded = jnp.pad(blocks, ((0, 0), (0, 0), (0, 0), (reach, reach), (0, 0)))
    shifted = jnp.stack(
        [
            lax.dynamic_slice_in_dim(padded, band_offsets[band_pos] + reach, NBLK, 3)
            for band_pos in range(BAND)
        ],
        axis=3,
    )
    products = jnp.einsum(
        "cfskbj,fbkpjl->pcfsbl", shifted, operator, preferred_element_type=jnp.float32
    )
    real_prod = products[0]
    imag_prod = products[1]
    src_real = real_prod[0] - imag_prod[1]
    src_imag = imag_prod[0] + real_prod[1]
    rec_real = real_prod[2] + imag_prod[3]
    rec_imag = real_prod[3] - imag_prod[2]
    joined = jnp.stack([src_real, src_imag, rec_real, rec_imag])
    return joined.reshape(nfield, freqs, slots, points).astype(jnp.bfloat16)


def fold_owners(partial_value, my_owner):
    for bit_pos in range(FOWNERS.bit_length() - 2, -1, -1):
        half_rows = partial_value.shape[-2] // 2
        lower_half = partial_value[..., :half_rows, :]
        upper_half = partial_value[..., half_rows:, :]
        upper_mine = my_owner // 2**bit_pos % 2 == 1
        outgoing = jnp.where(upper_mine, lower_half, upper_half)
        kept_half = jnp.where(upper_mine, upper_half, lower_half)
        partial_value = kept_half + from_partner(outgoing, "depth", bit_pos)
    return partial_value


def on_device(fronts, extrap, offsets, assign):
    dev_index = lax.axis_index("depth")
    my_section = dev_index // FOWNERS
    my_owner = dev_index % FOWNERS
    band_offsets = lax.dynamic_index_in_dim(offsets, my_section, 0, keepdims=False)
    my_assign = lax.dynamic_index_in_dim(assign, my_section, 0, keepdims=False)
    slot_count = fronts.shape[2]
    placing = (my_assign[:, None] == jnp.arange(slot_count, dtype=jnp.int32)[None, :]).astype(
        jnp.float32
    )
    image_scale = 1.0 / math.sqrt(2.0 * NFREQ)
    wave_state = fronts
    partials = []
    advanced = fronts
    for handover in range(HANDOVERS):
        more_rounds = handover + 1 < HANDOVERS
        advanced = advance(wave_state, band_offsets, extrap)
        if more_rounds:
            wave_state = passed_along(advanced, "depth", FOWNERS)
        fields = advanced.astype(jnp.float32)
        partial_value = image_scale * jnp.sum(fields[0] * fields[2] + fields[1] * fields[3], axis=0)
        placed = jnp.einsum("ji,jx->ix", placing, partial_value, precision=lax.Precision.HIGHEST)
        partials.append(fold_owners(placed, my_owner))
    images = jnp.stack(partials)
    return (images, advanced)


def solution(mesh):
    placed = (
        P(None, ("groups", "depth"), None, None),
        P("depth", None, None, None, None, None),
        P(),
        P(),
    )
    return jax.shard_map(
        on_device,
        mesh=mesh,
        in_specs=placed,
        out_specs=(P(None, ("groups", "depth"), None), P(None, ("groups", "depth"), None, None)),
        check_vma=False,
    )
```

profile of v0, /device:TPU:0, one launch (start us, length us, event | category | flops | bytes accessed | tf_op | source)
XLA Modules:
  0.0 180.5 jit_solution(8746024615223880882)
XLA Ops:
  9.6 5.0 %fusion.16 = f32[2,4,2,8,16,128]{5,3,0,1,4,2:T(8,128)S(1)} fusion(bf16[4,2,8,5,16,128]{5,2,3,0,4,1:T(8,128)(2,1)S(1)} %fusion.57, bf16[2,16,5,2,128,128]{5,4,3,2,1,0:T(8,128)(2,1)} %param.5), kind=kOutput, calls=%fused_computation.16 | convolution fusion | flops 335544320 | bytes 12845056 | tf_op jit(solution)/shard_map/cfskbj,fbkpjl->pcfsbl/dot_general | solution.py:39
  15.1 3.1 %collective-permute-start = (f32[4,2048]{1,0:T(4,128)S(1)}, f32[4,2048]{1,0:T(4,128)S(1)}, u32[]{:S(2)}, u32[]{:S(2)}) collective-permute-start(f32[4,2048]{1,0:T(4,128)S(1)} %slice_select_fusion.7), channel_id=1, source_target_pairs={{0,4},{1,5},{2,6},{3,7},{4,0},{5,1},{6,2},{7,3},{8,12},{9,13},{10,... | collective-permute-start | bytes 98312 | tf_op jit(solution)/shard_map/ppermute | solution.py:19
  22.2 2.6 %collective-permute-start.3 = (bf16[4,2,8,2048]{3,2,1,0:T(8,128)(2,1)S(1)}, bf16[4,2,8,2048]{3,2,1,0:T(8,128)(2,1)S(1)}, u32[]{:S(2)}, u32[]{:S(2)}) collective-permute-start(bf16[4,2,8,2048]{3,2,1,0:T(8,128)(2,1)S(1)} %get-tuple-element.83), channel_id=1, source_target_pairs={{0,8},{1,9},{2,10},{3,11},{4,12},{5,13},{6,14},{7,15},{8,0},{9,1},... | collective-permute-start | bytes 786440 | tf_op jit(solution)/shard_map/ppermute | solution.py:24
  24.8 10.5 %collective-permute-done.3 = bf16[4,2,8,2048]{3,2,1,0:T(8,128)(2,1)S(1)} collective-permute-done((bf16[4,2,8,2048]{3,2,1,0:T(8,128)(2,1)S(1)}, bf16[4,2,8,2048]{3,2,1,0:T(8,128)(2,1)S(1)}, u32[]{:S(2)}, u32[]{:S(2)}) %collective-permute-start.3) | collective-permute-done | bytes 262176 | tf_op jit(solution)/shard_map/ppermute | solution.py:24
  36.5 5.7 %fusion.19 = f32[2,4,2,8,16,128]{5,3,0,1,4,2:T(8,128)S(1)} fusion(bf16[4,2,8,5,16,128]{5,2,3,0,4,1:T(8,128)(2,1)S(1)} %bitcast_dynamic-update-slice_fusion.30, bf16[2,16,5,2,128,128]{5,4,3,2,1,0:T(8,128)(2,1)} %param.5), kind=kOutput, calls=%fused_computation.17 | convolution fusion | flops 335544320 | bytes 12845056 | tf_op jit(solution)/shard_map/cfskbj,fbkpjl->pcfsbl/dot_general | solution.py:39
  43.5 3.2 %collective-permute-done.4 = f32[4,2048]{1,0:T(4,128)S(1)} collective-permute-done((f32[4,2048]{1,0:T(4,128)S(1)}, f32[4,2048]{1,0:T(4,128)S(1)}, u32[]{:S(2)}, u32[]{:S(2)}) %collective-permute-start.4) | collective-permute-done | bytes 32800 | tf_op jit(solution)/shard_map/ppermute | solution.py:19
  47.3 2.2 %collective-permute-start.7 = (bf16[4,2,8,2048]{3,2,1,0:T(8,128)(2,1)S(1)}, bf16[4,2,8,2048]{3,2,1,0:T(8,128)(2,1)S(1)}, u32[]{:S(2)}, u32[]{:S(2)}) collective-permute-start(bf16[4,2,8,2048]{3,2,1,0:T(8,128)(2,1)S(1)} %get-tuple-element.76), channel_id=1, source_target_pairs={{0,8},{1,9},{2,10},{3,11},{4,12},{5,13},{6,14},{7,15},{8,0},{9,1},... | collective-permute-start | bytes 786440 | tf_op jit(solution)/shard_map/ppermute | solution.py:24
  50.6 9.9 %collective-permute-done.7 = bf16[4,2,8,2048]{3,2,1,0:T(8,128)(2,1)S(1)} collective-permute-done((bf16[4,2,8,2048]{3,2,1,0:T(8,128)(2,1)S(1)}, bf16[4,2,8,2048]{3,2,1,0:T(8,128)(2,1)S(1)}, u32[]{:S(2)}, u32[]{:S(2)}) %collective-permute-start.7) | collective-permute-done | bytes 262176 | tf_op jit(solution)/shard_map/ppermute | solution.py:24
  64.8 3.1 %collective-permute-done.8 = f32[4,2048]{1,0:T(4,128)S(1)} collective-permute-done((f32[4,2048]{1,0:T(4,128)S(1)}, f32[4,2048]{1,0:T(4,128)S(1)}, u32[]{:S(2)}, u32[]{:S(2)}) %collective-permute-start.8) | collective-permute-done | bytes 32800 | tf_op jit(solution)/shard_map/ppermute | solution.py:19
  69.5 2.1 %collective-permute-start.11 = (bf16[4,2,8,2048]{3,2,1,0:T(8,128)(2,1)S(1)}, bf16[4,2,8,2048]{3,2,1,0:T(8,128)(2,1)S(1)}, u32[]{:S(2)}, u32[]{:S(2)}) collective-permute-start(bf16[4,2,8,2048]{3,2,1,0:T(8,128)(2,1)S(1)} %get-tuple-element.69), channel_id=1, source_target_pairs={{0,8},{1,9},{2,10},{3,11},{4,12},{5,13},{6,14},{7,15},{8,0},{9,1},... | collective-permute-start | bytes 786440 | tf_op jit(solution)/shard_map/ppermute | solution.py:24
  71.7 10.8 %collective-permute-done.11 = bf16[4,2,8,2048]{3,2,1,0:T(8,128)(2,1)S(1)} collective-permute-done((bf16[4,2,8,2048]{3,2,1,0:T(8,128)(2,1)S(1)}, bf16[4,2,8,2048]{3,2,1,0:T(8,128)(2,1)S(1)}, u32[]{:S(2)}, u32[]{:S(2)}) %collective-permute-start.11) | collective-permute-done | bytes 262176 | tf_op jit(solution)/shard_map/ppermute | solution.py:24
  86.9 3.1 %collective-permute-done.12 = f32[4,2048]{1,0:T(4,128)S(1)} collective-permute-done((f32[4,2048]{1,0:T(4,128)S(1)}, f32[4,2048]{1,0:T(4,128)S(1)}, u32[]{:S(2)}, u32[]{:S(2)}) %collective-permute-start.12) | collective-permute-done | bytes 32800 | tf_op jit(solution)/shard_map/ppermute | solution.py:19
  90.6 2.1 %collective-permute-start.15 = (bf16[4,2,8,2048]{3,2,1,0:T(8,128)(2,1)S(1)}, bf16[4,2,8,2048]{3,2,1,0:T(8,128)(2,1)S(1)}, u32[]{:S(2)}, u32[]{:S(2)}) collective-permute-start(bf16[4,2,8,2048]{3,2,1,0:T(8,128)(2,1)S(1)} %get-tuple-element.62), channel_id=1, source_target_pairs={{0,8},{1,9},{2,10},{3,11},{4,12},{5,13},{6,14},{7,15},{8,0},{9,1},... | collective-permute-start | bytes 786440 | tf_op jit(solution)/shard_map/ppermute | solution.py:24
  93.8 9.9 %collective-permute-done.15 = bf16[4,2,8,2048]{3,2,1,0:T(8,128)(2,1)S(1)} collective-permute-done((bf16[4,2,8,2048]{3,2,1,0:T(8,128)(2,1)S(1)}, bf16[4,2,8,2048]{3,2,1,0:T(8,128)(2,1)S(1)}, u32[]{:S(2)}, u32[]{:S(2)}) %collective-permute-start.15) | collective-permute-done | bytes 262176 | tf_op jit(solution)/shard_map/ppermute | solution.py:24
  108.0 3.1 %collective-permute-done.16 = f32[4,2048]{1,0:T(4,128)S(1)} collective-permute-done((f32[4,2048]{1,0:T(4,128)S(1)}, f32[4,2048]{1,0:T(4,128)S(1)}, u32[]{:S(2)}, u32[]{:S(2)}) %collective-permute-start.16) | collective-permute-done | bytes 32800 | tf_op jit(solution)/shard_map/ppermute | solution.py:19
  112.7 2.1 %collective-permute-start.19 = (bf16[4,2,8,2048]{3,2,1,0:T(8,128)(2,1)S(1)}, bf16[4,2,8,2048]{3,2,1,0:T(8,128)(2,1)S(1)}, u32[]{:S(2)}, u32[]{:S(2)}) collective-permute-start(bf16[4,2,8,2048]{3,2,1,0:T(8,128)(2,1)S(1)} %get-tuple-element.55), channel_id=1, source_target_pairs={{0,8},{1,9},{2,10},{3,11},{4,12},{5,13},{6,14},{7,15},{8,0},{9,1},... | collective-permute-start | bytes 786440 | tf_op jit(solution)/shard_map/ppermute | solution.py:24
  115.0 10.8 %collective-permute-done.19 = bf16[4,2,8,2048]{3,2,1,0:T(8,128)(2,1)S(1)} collective-permute-done((bf16[4,2,8,2048]{3,2,1,0:T(8,128)(2,1)S(1)}, bf16[4,2,8,2048]{3,2,1,0:T(8,128)(2,1)S(1)}, u32[]{:S(2)}, u32[]{:S(2)}) %collective-permute-start.19) | collective-permute-done | bytes 262176 | tf_op jit(solution)/shard_map/ppermute | solution.py:24
  130.3 3.1 %collective-permute-done.20 = f32[4,2048]{1,0:T(4,128)S(1)} collective-permute-done((f32[4,2048]{1,0:T(4,128)S(1)}, f32[4,2048]{1,0:T(4,128)S(1)}, u32[]{:S(2)}, u32[]{:S(2)}) %collective-permute-start.20) | collective-permute-done | bytes 32800 | tf_op jit(solution)/shard_map/ppermute | solution.py:19
  134.1 2.1 %collective-permute-start.23 = (bf16[4,2,8,2048]{3,2,1,0:T(8,128)(2,1)S(1)}, bf16[4,2,8,2048]{3,2,1,0:T(8,128)(2,1)S(1)}, u32[]{:S(2)}, u32[]{:S(2)}) collective-permute-start(bf16[4,2,8,2048]{3,2,1,0:T(8,128)(2,1)S(1)} %get-tuple-element.48), channel_id=1, source_target_pairs={{0,8},{1,9},{2,10},{3,11},{4,12},{5,13},{6,14},{7,15},{8,0},{9,1},... | collective-permute-start | bytes 786440 | tf_op jit(solution)/shard_map/ppermute | solution.py:24
  137.4 9.8 %collective-permute-done.23 = bf16[4,2,8,2048]{3,2,1,0:T(8,128)(2,1)S(1)} collective-permute-done((bf16[4,2,8,2048]{3,2,1,0:T(8,128)(2,1)S(1)}, bf16[4,2,8,2048]{3,2,1,0:T(8,128)(2,1)S(1)}, u32[]{:S(2)}, u32[]{:S(2)}) %collective-permute-start.23) | collective-permute-done | bytes 262176 | tf_op jit(solution)/shard_map/ppermute | solution.py:24
  151.4 3.4 %collective-permute-start.27 = (bf16[4,2,8,2048]{3,2,1,0:T(8,128)(2,1)S(1)}, bf16[4,2,8,2048]{3,2,1,0:T(8,128)(2,1)S(1)}, u32[]{:S(2)}, u32[]{:S(2)}) collective-permute-start(bf16[4,2,8,2048]{3,2,1,0:T(8,128)(2,1)S(1)} %get-tuple-element.41), channel_id=1, source_target_pairs={{0,8},{1,9},{2,10},{3,11},{4,12},{5,13},{6,14},{7,15},{8,0},{9,1},... | collective-permute-start | bytes 786440 | tf_op jit(solution)/shard_map/ppermute | solution.py:24
  156.4 10.2 %collective-permute-done.27 = bf16[4,2,8,2048]{3,2,1,0:T(8,128)(2,1)S(1)} collective-permute-done((bf16[4,2,8,2048]{3,2,1,0:T(8,128)(2,1)S(1)}, bf16[4,2,8,2048]{3,2,1,0:T(8,128)(2,1)S(1)}, u32[]{:S(2)}, u32[]{:S(2)}) %collective-permute-start.27) | collective-permute-done | bytes 262176 | tf_op jit(solution)/shard_map/ppermute | solution.py:24
  170.9 3.9 %collective-permute-done.28 = f32[4,2048]{1,0:T(4,128)S(1)} collective-permute-done((f32[4,2048]{1,0:T(4,128)S(1)}, f32[4,2048]{1,0:T(4,128)S(1)}, u32[]{:S(2)}, u32[]{:S(2)}) %collective-permute-start.28) | collective-permute-done | bytes 32800 | tf_op jit(solution)/shard_map/ppermute | solution.py:19
  176.4 2.2 %collective-permute-done.29 = f32[2,2048]{1,0:T(2,128)S(1)} collective-permute-done((f32[2,2048]{1,0:T(2,128)S(1)}, f32[2,2048]{1,0:T(2,128)S(1)}, u32[]{:S(2)}, u32[]{:S(2)}) %collective-permute-start.29) | collective-permute-done | bytes 16416 | tf_op jit(solution)/shard_map/ppermute | solution.py:19
  (194 shorter events, 48.2 us)
Async XLA Ops:
  15.1 5.0 %collective-permute-start = (f32[4,2048]{1,0:T(4,128)S(1)}, f32[4,2048]{1,0:T(4,128)S(1)}, u32[]{:S(2)}, u32[]{:S(2)}) collective-permute-start(f32[4,2048]{1,0:T(4,128)S(1)} %slice_select_fusion.7), channel_id=1, source_target_pairs={{0,4},{1,5},{2,6},{3,7},{4,0},{5,1},{6,2},{7,3},{8,12},{9,13},{10,... | collective-permute-start | bytes 98312 | tf_op jit(solution)/shard_map/ppermute | solution.py:19
  20.1 4.6 %collective-permute-start.1 = (f32[2,2048]{1,0:T(2,128)S(1)}, f32[2,2048]{1,0:T(2,128)S(1)}, u32[]{:S(2)}, u32[]{:S(2)}) collective-permute-start(f32[2,2048]{1,0:T(2,128)S(1)} %broadcast_select_fusion.7), channel_id=1, source_target_pairs={{0,2},{1,3},{2,0},{3,1},{4,6},{5,7},{6,4},{7,5},{8,10},{9,11},{10,... | collective-permute-start | bytes 49160 | tf_op jit(solution)/shard_map/ppermute | solution.py:19
  22.2 13.1 %collective-permute-start.3 = (bf16[4,2,8,2048]{3,2,1,0:T(8,128)(2,1)S(1)}, bf16[4,2,8,2048]{3,2,1,0:T(8,128)(2,1)S(1)}, u32[]{:S(2)}, u32[]{:S(2)}) collective-permute-start(bf16[4,2,8,2048]{3,2,1,0:T(8,128)(2,1)S(1)} %get-tuple-element.83), channel_id=1, source_target_pairs={{0,8},{1,9},{2,10},{3,11},{4,12},{5,13},{6,14},{7,15},{8,0},{9,1},... | collective-permute-start | bytes 786440 | tf_op jit(solution)/shard_map/ppermute | solution.py:24
  42.7 4.0 %collective-permute-start.4 = (f32[4,2048]{1,0:T(4,128)S(1)}, f32[4,2048]{1,0:T(4,128)S(1)}, u32[]{:S(2)}, u32[]{:S(2)}) collective-permute-start(f32[4,2048]{1,0:T(4,128)S(1)} %slice_select_fusion.6), channel_id=1, source_target_pairs={{0,4},{1,5},{2,6},{3,7},{4,0},{5,1},{6,2},{7,3},{8,12},{9,13},{10,... | collective-permute-start | bytes 98312 | tf_op jit(solution)/shard_map/ppermute | solution.py:19
  46.7 3.8 %collective-permute-start.5 = (f32[2,2048]{1,0:T(2,128)S(1)}, f32[2,2048]{1,0:T(2,128)S(1)}, u32[]{:S(2)}, u32[]{:S(2)}) collective-permute-start(f32[2,2048]{1,0:T(2,128)S(1)} %broadcast_select_fusion.6), channel_id=1, source_target_pairs={{0,2},{1,3},{2,0},{3,1},{4,6},{5,7},{6,4},{7,5},{8,10},{9,11},{10,... | collective-permute-start | bytes 49160 | tf_op jit(solution)/shard_map/ppermute | solution.py:19
  47.3 13.2 %collective-permute-start.7 = (bf16[4,2,8,2048]{3,2,1,0:T(8,128)(2,1)S(1)}, bf16[4,2,8,2048]{3,2,1,0:T(8,128)(2,1)S(1)}, u32[]{:S(2)}, u32[]{:S(2)}) collective-permute-start(bf16[4,2,8,2048]{3,2,1,0:T(8,128)(2,1)S(1)} %get-tuple-element.76), channel_id=1, source_target_pairs={{0,8},{1,9},{2,10},{3,11},{4,12},{5,13},{6,14},{7,15},{8,0},{9,1},... | collective-permute-start | bytes 786440 | tf_op jit(solution)/shard_map/ppermute | solution.py:24
  63.9 4.0 %collective-permute-start.8 = (f32[4,2048]{1,0:T(4,128)S(1)}, f32[4,2048]{1,0:T(4,128)S(1)}, u32[]{:S(2)}, u32[]{:S(2)}) collective-permute-start(f32[4,2048]{1,0:T(4,128)S(1)} %slice_select_fusion.5), channel_id=1, source_target_pairs={{0,4},{1,5},{2,6},{3,7},{4,0},{5,1},{6,2},{7,3},{8,12},{9,13},{10,... | collective-permute-start | bytes 98312 | tf_op jit(solution)/shard_map/ppermute | solution.py:19
  64.7 4.8 %collective-permute-start.6 = (f32[1,2048]{1,0:T(1,128)S(1)}, f32[1,2048]{1,0:T(1,128)S(1)}, u32[]{:S(2)}, u32[]{:S(2)}) collective-permute-start(f32[1,2048]{1,0:T(1,128)S(1)} %broadcast_select_fusion.20), channel_id=1, source_target_pairs={{0,1},{1,0},{2,3},{3,2},{4,5},{5,4},{6,7},{7,6},{8,9},{9,8},{10,11... | collective-permute-start | bytes 24584 | tf_op jit(solution)/shard_map/ppermute | solution.py:19
  69.5 13.1 %collective-permute-start.11 = (bf16[4,2,8,2048]{3,2,1,0:T(8,128)(2,1)S(1)}, bf16[4,2,8,2048]{3,2,1,0:T(8,128)(2,1)S(1)}, u32[]{:S(2)}, u32[]{:S(2)}) collective-permute-start(bf16[4,2,8,2048]{3,2,1,0:T(8,128)(2,1)S(1)} %get-tuple-element.69), channel_id=1, source_target_pairs={{0,8},{1,9},{2,10},{3,11},{4,12},{5,13},{6,14},{7,15},{8,0},{9,1},... | collective-permute-start | bytes 786440 | tf_op jit(solution)/shard_map/ppermute | solution.py:24
  86.0 4.0 %collective-permute-start.12 = (f32[4,2048]{1,0:T(4,128)S(1)}, f32[4,2048]{1,0:T(4,128)S(1)}, u32[]{:S(2)}, u32[]{:S(2)}) collective-permute-start(f32[4,2048]{1,0:T(4,128)S(1)} %slice_select_fusion.4), channel_id=1, source_target_pairs={{0,4},{1,5},{2,6},{3,7},{4,0},{5,1},{6,2},{7,3},{8,12},{9,13},{10,... | collective-permute-start | bytes 98312 | tf_op jit(solution)/shard_map/ppermute | solution.py:19
  86.8 3.8 %collective-permute-start.10 = (f32[1,2048]{1,0:T(1,128)S(1)}, f32[1,2048]{1,0:T(1,128)S(1)}, u32[]{:S(2)}, u32[]{:S(2)}) collective-permute-start(f32[1,2048]{1,0:T(1,128)S(1)} %broadcast_select_fusion.18), channel_id=1, source_target_pairs={{0,1},{1,0},{2,3},{3,2},{4,5},{5,4},{6,7},{7,6},{8,9},{9,8},{10,11... | collective-permute-start | bytes 24584 | tf_op jit(solution)/shard_map/ppermute | solution.py:19
  90.6 13.1 %collective-permute-start.15 = (bf16[4,2,8,2048]{3,2,1,0:T(8,128)(2,1)S(1)}, bf16[4,2,8,2048]{3,2,1,0:T(8,128)(2,1)S(1)}, u32[]{:S(2)}, u32[]{:S(2)}) collective-permute-start(bf16[4,2,8,2048]{3,2,1,0:T(8,128)(2,1)S(1)} %get-tuple-element.62), channel_id=1, source_target_pairs={{0,8},{1,9},{2,10},{3,11},{4,12},{5,13},{6,14},{7,15},{8,0},{9,1},... | collective-permute-start | bytes 786440 | tf_op jit(solution)/shard_map/ppermute | solution.py:24
  107.1 4.0 %collective-permute-start.16 = (f32[4,2048]{1,0:T(4,128)S(1)}, f32[4,2048]{1,0:T(4,128)S(1)}, u32[]{:S(2)}, u32[]{:S(2)}) collective-permute-start(f32[4,2048]{1,0:T(4,128)S(1)} %slice_select_fusion.3), channel_id=1, source_target_pairs={{0,4},{1,5},{2,6},{3,7},{4,0},{5,1},{6,2},{7,3},{8,12},{9,13},{10,... | collective-permute-start | bytes 98312 | tf_op jit(solution)/shard_map/ppermute | solution.py:19
  107.9 4.8 %collective-permute-start.14 = (f32[1,2048]{1,0:T(1,128)S(1)}, f32[1,2048]{1,0:T(1,128)S(1)}, u32[]{:S(2)}, u32[]{:S(2)}) collective-permute-start(f32[1,2048]{1,0:T(1,128)S(1)} %broadcast_select_fusion.16), channel_id=1, source_target_pairs={{0,1},{1,0},{2,3},{3,2},{4,5},{5,4},{6,7},{7,6},{8,9},{9,8},{10,11... | collective-permute-start | bytes 24584 | tf_op jit(solution)/shard_map/ppermute | solution.py:19
  112.7 13.1 %collective-permute-start.19 = (bf16[4,2,8,2048]{3,2,1,0:T(8,128)(2,1)S(1)}, bf16[4,2,8,2048]{3,2,1,0:T(8,128)(2,1)S(1)}, u32[]{:S(2)}, u32[]{:S(2)}) collective-permute-start(bf16[4,2,8,2048]{3,2,1,0:T(8,128)(2,1)S(1)} %get-tuple-element.55), channel_id=1, source_target_pairs={{0,8},{1,9},{2,10},{3,11},{4,12},{5,13},{6,14},{7,15},{8,0},{9,1},... | collective-permute-start | bytes 786440 | tf_op jit(solution)/shard_map/ppermute | solution.py:24
  129.4 4.0 %collective-permute-start.20 = (f32[4,2048]{1,0:T(4,128)S(1)}, f32[4,2048]{1,0:T(4,128)S(1)}, u32[]{:S(2)}, u32[]{:S(2)}) collective-permute-start(f32[4,2048]{1,0:T(4,128)S(1)} %slice_select_fusion.2), channel_id=1, source_target_pairs={{0,4},{1,5},{2,6},{3,7},{4,0},{5,1},{6,2},{7,3},{8,12},{9,13},{10,... | collective-permute-start | bytes 98312 | tf_op jit(solution)/shard_map/ppermute | solution.py:19
  130.2 3.8 %collective-permute-start.18 = (f32[1,2048]{1,0:T(1,128)S(1)}, f32[1,2048]{1,0:T(1,128)S(1)}, u32[]{:S(2)}, u32[]{:S(2)}) collective-permute-start(f32[1,2048]{1,0:T(1,128)S(1)} %broadcast_select_fusion.14), channel_id=1, source_target_pairs={{0,1},{1,0},{2,3},{3,2},{4,5},{5,4},{6,7},{7,6},{8,9},{9,8},{10,11... | collective-permute-start | bytes 24584 | tf_op jit(solution)/shard_map/ppermute | solution.py:19
  133.5 3.8 %collective-permute-start.21 = (f32[2,2048]{1,0:T(2,128)S(1)}, f32[2,2048]{1,0:T(2,128)S(1)}, u32[]{:S(2)}, u32[]{:S(2)}) collective-permute-start(f32[2,2048]{1,0:T(2,128)S(1)} %broadcast_select_fusion.2), channel_id=1, source_target_pairs={{0,2},{1,3},{2,0},{3,1},{4,6},{5,7},{6,4},{7,5},{8,10},{9,11},{10,... | collective-permute-start | bytes 49160 | tf_op jit(solution)/shard_map/ppermute | solution.py:19
  134.1 13.1 %collective-permute-start.23 = (bf16[4,2,8,2048]{3,2,1,0:T(8,128)(2,1)S(1)}, bf16[4,2,8,2048]{3,2,1,0:T(8,128)(2,1)S(1)}, u32[]{:S(2)}, u32[]{:S(2)}) collective-permute-start(bf16[4,2,8,2048]{3,2,1,0:T(8,128)(2,1)S(1)} %get-tuple-element.48), channel_id=1, source_target_pairs={{0,8},{1,9},{2,10},{3,11},{4,12},{5,13},{6,14},{7,15},{8,0},{9,1},... | collective-permute-start | bytes 786440 | tf_op jit(solution)/shard_map/ppermute | solution.py:24
  137.3 14.1 %collective-permute-start.22 = (f32[1,2048]{1,0:T(1,128)S(1)}, f32[1,2048]{1,0:T(1,128)S(1)}, u32[]{:S(2)}, u32[]{:S(2)}) collective-permute-start(f32[1,2048]{1,0:T(1,128)S(1)} %broadcast_select_fusion.12), channel_id=1, source_target_pairs={{0,1},{1,0},{2,3},{3,2},{4,5},{5,4},{6,7},{7,6},{8,9},{9,8},{10,11... | collective-permute-start | bytes 24584 | tf_op jit(solution)/shard_map/ppermute | solution.py:19
  150.6 4.3 %collective-permute-start.24 = (f32[4,2048]{1,0:T(4,128)S(1)}, f32[4,2048]{1,0:T(4,128)S(1)}, u32[]{:S(2)}, u32[]{:S(2)}) collective-permute-start(f32[4,2048]{1,0:T(4,128)S(1)} %slice_select_fusion.1), channel_id=1, source_target_pairs={{0,4},{1,5},{2,6},{3,7},{4,0},{5,1},{6,2},{7,3},{8,12},{9,13},{10,... | collective-permute-start | bytes 98312 | tf_op jit(solution)/shard_map/ppermute | solution.py:19
  151.4 15.2 %collective-permute-start.27 = (bf16[4,2,8,2048]{3,2,1,0:T(8,128)(2,1)S(1)}, bf16[4,2,8,2048]{3,2,1,0:T(8,128)(2,1)S(1)}, u32[]{:S(2)}, u32[]{:S(2)}) collective-permute-start(bf16[4,2,8,2048]{3,2,1,0:T(8,128)(2,1)S(1)} %get-tuple-element.41), channel_id=1, source_target_pairs={{0,8},{1,9},{2,10},{3,11},{4,12},{5,13},{6,14},{7,15},{8,0},{9,1},... | collective-permute-start | bytes 786440 | tf_op jit(solution)/shard_map/ppermute | solution.py:24
  154.9 15.9 %collective-permute-start.25 = (f32[2,2048]{1,0:T(2,128)S(1)}, f32[2,2048]{1,0:T(2,128)S(1)}, u32[]{:S(2)}, u32[]{:S(2)}) collective-permute-start(f32[2,2048]{1,0:T(2,128)S(1)} %broadcast_select_fusion.1), channel_id=1, source_target_pairs={{0,2},{1,3},{2,0},{3,1},{4,6},{5,7},{6,4},{7,5},{8,10},{9,11},{10,... | collective-permute-start | bytes 49160 | tf_op jit(solution)/shard_map/ppermute | solution.py:19
  170.8 4.0 %collective-permute-start.28 = (f32[4,2048]{1,0:T(4,128)S(1)}, f32[4,2048]{1,0:T(4,128)S(1)}, u32[]{:S(2)}, u32[]{:S(2)}) collective-permute-start(f32[4,2048]{1,0:T(4,128)S(1)} %slice_select_fusion), channel_id=1, source_target_pairs={{0,4},{1,5},{2,6},{3,7},{4,0},{5,1},{6,2},{7,3},{8,12},{9,13},{10,... | collective-permute-start | bytes 98312 | tf_op jit(solution)/shard_map/ppermute | solution.py:19
  (12 other events, 101.4 us)
where the time goes:
time: 181 us
  waiting for transfers between devices  100 us (55%)
  starting transfers between devices  35.1 us (19%)
  matrix products  23.5 us (13%)
  local copies, waits for them, and re-layouts  11.2 us (6%)
  between operations  8.08 us (4%)
  other arithmetic  2.56 us (1%)
    ppermute x7, waiting for transfers between devices, passed_along(): lax.ppermute(shard, axis, [(i, (i + by) % size) for i in range(size)])  72 us
    ppermute x24, waiting for transfers between devices, from_partner(): return lax.ppermute(value, axis, pairs)  28 us
    dot_general x8, matrix products, advance(): jnp.einsum('cfskbj,fbkpjl->pcfsbl', shifted, operator, preferred_element_...  21.2 us
    ppermute x24, starting transfers between devices, from_partner(): return lax.ppermute(value, axis, pairs)  18.3 us
    ppermute x7, starting transfers between devices, passed_along(): lax.ppermute(shard, axis, [(i, (i + by) % size) for i in range(size)])  16.8 us
    unnamed x49, local copies, waits for them, and re-layouts  4.16 us
    dynamic_slice x7, local copies, waits for them, and re-layouts, advance(): lax.dynamic_slice_in_dim(padded, band_offsets[band_pos] + reach, NBLK, 3)  4.13 us
  transfers between devices with their start and end apart: 31, of which 21 were waited for; matrix products, arithmetic and copies ran while one was open for 4% of the time, Pallas kernels for 0%

commit v1 on v0

v1 whole, which is shorter than its diff:
```python
import functools
import math

import jax
import jax.numpy as jnp
from jax import lax
from jax.experimental import pallas as pl
from jax.experimental.pallas import tpu as pltpu
from jax.sharding import PartitionSpec as P

HANDOVERS = 8
CHUNKS = 4
MESH = pl.DeviceIdType.MESH


def kernel(
    sections,
    owners,
    offsets_ref,
    assign_ref,
    fronts_ref,
    extrap_ref,
    images_ref,
    last_ref,
    oper,
    padded,
    outbox,
    inbox,
    half_image,
    slot_image,
    image_out,
    image_in,
    load_sem,
    wave_send,
    wave_recv,
    image_send,
    image_recv,
):
    nfield, freqs, slots, _ = fronts_ref.shape
    nblk, band, block = extrap_ref.shape[1], extrap_ref.shape[2], extrap_ref.shape[-1]
    reach = band // 2
    per_chunk = nblk // CHUNKS
    scale = 1.0 / math.sqrt(2.0 * freqs * owners)
    me = lax.axis_index("depth")
    depth = sections * owners
    section = me // owners
    owner = me % owners
    ahead = (me + owners) % depth
    behind = (me + depth - owners) % depth

    def load(freq, chunk):
        rows = pl.ds(chunk * per_chunk, per_chunk)
        return pltpu.make_async_copy(
            extrap_ref.at[freq, rows], oper.at[freq, rows], load_sem.at[freq, chunk]
        )

    for freq in range(freqs):
        for chunk in range(CHUNKS):
            load(freq, chunk).start()

    def mate(step):
        return section * owners + (owner + step) % owners

    barrier = pltpu.get_barrier_semaphore()
    greeted = [ahead] + ([behind] if sections > 2 else []) + [mate(d) for d in range(1, owners)]
    for device in greeted:
        pl.semaphore_signal(barrier, inc=1, device_id={"depth": device}, device_id_type=MESH)

    offs = [offsets_ref[section, k] + reach for k in range(band)]
    slot_of = []
    for shot in range(slots):
        found = jnp.int32(0)
        for slot in range(slots):
            found = jnp.where(assign_ref[section, slot] == shot, slot, found)
        slot_of.append(found)

    blank = jnp.zeros((reach,) + padded.shape[2:], padded.dtype)
    for freq in range(freqs):
        padded[freq, 0:reach] = blank
        padded[freq, reach + nblk : 2 * reach + nblk] = blank
        for b in range(nblk):
            cols = slice(b * block, (b + 1) * block)
            rows = [fronts_ref[c, freq, :, cols].astype(jnp.float32) for c in range(nfield)]
            padded[freq, reach + b] = jnp.concatenate(rows, axis=0).astype(padded.dtype)

    def wave_copy(rnd, freq, rows):
        return pltpu.make_async_remote_copy(
            src_ref=outbox.at[rnd, freq, rows],
            dst_ref=inbox.at[rnd, freq, rows],
            send_sem=wave_send.at[rnd, freq],
            recv_sem=wave_recv.at[rnd, freq],
            device_id={"depth": ahead},
            device_id_type=MESH,
        )

    def image_copy(rnd, step):
        return pltpu.make_async_remote_copy(
            src_ref=image_out.at[rnd, step],
            dst_ref=image_in.at[rnd, step],
            send_sem=image_send.at[rnd],
            recv_sem=image_recv.at[rnd],
            device_id={"depth": mate(step)},
            device_id_type=MESH,
        )

    def image_all(rnd):
        return pltpu.make_async_remote_copy(
            src_ref=image_out.at[rnd, pl.ds(1, owners - 1)],
            dst_ref=image_in.at[rnd, pl.ds(1, owners - 1)],
            send_sem=image_send.at[rnd],
            recv_sem=image_recv.at[rnd],
            device_id={"depth": ahead},
            device_id_type=MESH,
        )

    def one_block(rnd, freq, b, last):
        lhs = jnp.concatenate([padded[freq, b + offs[k]] for k in range(band)], axis=1)
        rhs = jnp.concatenate(
            [
                jnp.concatenate([oper[freq, b, k, 0], oper[freq, b, k, 1]], axis=1)
                for k in range(band)
            ],
            axis=0,
        )
        both = jnp.dot(lhs, rhs, preferred_element_type=jnp.float32)
        re = [both[c * slots : (c + 1) * slots, :block] for c in range(nfield)]
        im = [both[c * slots : (c + 1) * slots, block:] for c in range(nfield)]
        new = [re[0] - im[1], im[0] + re[1], re[2] + im[3], re[3] - im[2]]
        rounded = jnp.concatenate(new, axis=0).astype(jnp.bfloat16)
        if last:
            cols = pl.ds(pl.multiple_of(b * block, block), block)
            for c in range(nfield):
                last_ref[c, freq, :, cols] = new[c].astype(jnp.bfloat16)
        else:
            outbox[rnd, freq, b] = rounded
        wide = rounded.astype(jnp.float32)
        part = [wide[c * slots : (c + 1) * slots] for c in range(nfield)]
        image = part[0] * part[2] + part[1] * part[3]
        if freq > 0:
            image = image + half_image[b]
        if freq < freqs - 1:
            half_image[b] = image
        else:
            for slot in range(slots):
                slot_image[slot, pl.ds(b, 1), :] = image[slot : slot + 1] * scale

    def advance(rnd, first=False, last=False):
        for freq in range(freqs):
            if not first:
                wave_copy(rnd - 1, freq, pl.ds(0, nblk)).wait_recv()
                padded[freq, reach : reach + nblk] = inbox[rnd - 1, freq]

            def chunk_body(chunk):
                if first:
                    load(freq, chunk).wait()
                for i in range(per_chunk):
                    one_block(rnd, freq, chunk * per_chunk + i, last)
                if first and freq == 0 and chunk == 0:
                    pl.semaphore_wait(barrier, len(greeted))
                if not last:
                    wave_copy(rnd, freq, pl.ds(chunk * per_chunk, per_chunk)).start()

            if first:
                for chunk in range(CHUNKS):
                    chunk_body(chunk)
            else:
                pl.loop(0, CHUNKS)(chunk_body)
        for step in range(owners):
            target = (owner + step) % owners
            chosen = slot_of[0]
            for shot in range(1, slots):
                chosen = jnp.where(target == shot, slot_of[shot], chosen)
            image_out[rnd, step] = slot_image[chosen]
        for step in range(1, owners):
            image_copy(rnd, step).start()

    def finish_image(rnd):
        image_all(rnd).wait_recv()
        total = image_out[rnd, 0]
        for step in range(1, owners):
            total = total + image_in[rnd, step]
        images_ref[rnd] = total

    advance(0, first=True)

    @pl.loop(1, HANDOVERS - 1)
    def _(rnd):
        advance(rnd)
        finish_image(rnd - 1)

    advance(HANDOVERS - 1, last=True)
    finish_image(HANDOVERS - 2)

    @pl.loop(0, HANDOVERS - 1)
    def _(rnd):
        for freq in range(freqs):
            wave_copy(rnd, freq, pl.ds(0, nblk)).wait_send()
        image_all(rnd).wait_send()

    finish_image(HANDOVERS - 1)
    image_all(HANDOVERS - 1).wait_send()


def on_device(sections, owners, fronts, extrap, offsets, assign):
    nfield, freqs, slots, points = fronts.shape
    _, nblk, band, _, block, _ = extrap.shape
    moves = HANDOVERS - 1
    wave = (moves, freqs, nblk, nfield * slots, block)
    image = (HANDOVERS, owners, nblk, block)
    vmem = pl.BlockSpec(memory_space=pltpu.VMEM)
    smem = pl.BlockSpec(memory_space=pltpu.SMEM)
    images, last = pl.pallas_call(
        functools.partial(kernel, sections, owners),
        out_shape=(
            jax.ShapeDtypeStruct((HANDOVERS, nblk, block), jnp.float32),
            jax.ShapeDtypeStruct(fronts.shape, fronts.dtype),
        ),
        in_specs=[smem, smem, vmem, pl.BlockSpec(memory_space=pl.ANY)],
        out_specs=(vmem, vmem),
        scratch_shapes=[
            pltpu.VMEM(extrap.shape, extrap.dtype),
            pltpu.VMEM((freqs, nblk + 2 * (band // 2), nfield * slots, block), fronts.dtype),
            pltpu.VMEM(wave, fronts.dtype),
            pltpu.VMEM(wave, fronts.dtype),
            pltpu.VMEM((nblk, slots, block), jnp.float32),
            pltpu.VMEM((slots, nblk, block), jnp.float32),
            pltpu.VMEM(image, jnp.float32),
            pltpu.VMEM(image, jnp.float32),
            pltpu.SemaphoreType.DMA((freqs, CHUNKS)),
            pltpu.SemaphoreType.DMA((moves, freqs)),
            pltpu.SemaphoreType.DMA((moves, freqs)),
            pltpu.SemaphoreType.DMA((HANDOVERS,)),
            pltpu.SemaphoreType.DMA((HANDOVERS,)),
        ],
        compiler_params=pltpu.CompilerParams(collective_id=0, has_side_effects=True),
    )(offsets, assign, fronts, extrap)
    return images.reshape(HANDOVERS, slots // owners, points), last


def solution(mesh):
    depth = mesh.shape["depth"]

    def program(fronts, extrap, offsets, assign):
        sections = offsets.shape[0]
        placed = (
            P(None, ("groups", "depth"), None, None),
            P("depth", None, None, None, None, None),
            P(),
            P(),
        )
        return jax.shard_map(
            functools.partial(on_device, sections, depth // sections),
            mesh=mesh,
            in_specs=placed,
            out_specs=(
                P(None, ("groups", "depth"), None),
                P(None, ("groups", "depth"), None, None),
            ),
            check_vma=False,
        )(fronts, extrap, offsets, assign)

    return program
```

time: 181 us -> 99.1 us (0.55)
  waiting for transfers between devices: 100 us -> 0 us
  Pallas kernels: 0 us -> 95.1 us
  starting transfers between devices: 35.1 us -> 0 us
  matrix products: 23.5 us -> 0 us
  local copies, waits for them, and re-layouts: 11.2 us -> 3.14 us
  between operations: 8.08 us -> 0.64 us
  other arithmetic: 2.56 us -> 0 us
    ppermute x31 -> x0, waiting for transfers between devices: 100 us -> none  [the longest x7 72 us: passed_along(): lax.ppermute(shard, axis, [(i, (i + by) % size) for i in range(size)])]
    pallas_call x0 -> x1, Pallas kernels: none -> 95.1 us  [on_device(): pl.pallas_call(functools.partial(kernel, sections, owners), out_shape=(ja...]
    ppermute x31 -> x0, starting transfers between devices: 35.1 us -> none  [the longest x24 18.3 us: from_partner(): return lax.ppermute(value, axis, pairs)]
    dot_general x16 -> x0, matrix products: 23.5 us -> none  [the longest x8 21.2 us: advance(): jnp.einsum('cfskbj,fbkpjl->pcfsbl', shifted, operator, preferred_element_...]
    dynamic_slice x8 -> x0, local copies, waits for them, and re-layouts: 4.85 us -> none  [the longest x7 4.13 us: advance(): lax.dynamic_slice_in_dim(padded, band_offsets[band_pos] + reach, NBLK, 3)]
    unnamed x49 -> x2, local copies, waits for them, and re-layouts: 4.16 us -> 3.14 us
  transfers between devices with their start and end apart: 31 -> 0, of which waited for: 21 -> 0; matrix products, arithmetic and copies ran while one was open for 4% -> 0% of each run, Pallas kernels for 0% -> 0%
where the time goes in v1:
time: 99.1 us; the launch traced here: 98.9 us
  Pallas kernels  95.1 us (96%)
  local copies, waits for them, and re-layouts  3.14 us (3%)
    pallas_call x1, Pallas kernels, on_device(): pl.pallas_call(functools.partial(kernel, sections, owners), out_shape=(ja...  95.1 us
    unnamed x2, local copies, waits for them, and re-layouts  3.14 us

profile of v1, /device:TPU:0, one launch (start us, length us, event | category | flops | bytes accessed | tf_op | source)
XLA Modules:
  0.0 98.9 jit_solution(3723166424821470895)
XLA Ops:
  0.6 95.1 %shard_map.59 = (f32[8,16,128]{2,1,0:T(8,128)}, bf16[4,2,8,2048]{3,2,1,0:T(8,128)(2,1)}) custom-call(s32[2,5]{1,0:T(2,128)} %offsets_ref.1, s32[2,8]{1,0:T(2,128)} %assign_ref.1, bf16[4,2,8,2048]{3,2,1,0:T(8,128)(2,1)} %fronts_ref.1, bf16[2,16,5,2,128,128]{5,4,3,2,1,0:T(8,128)(2,1)} %extrap_ref.1), custom_call_target="tpu_custom_call" | custom-call | tf_op jit(solution)/shard_map/pallas_call | solution.py:212
  95.7 1.5 %copy.9 = f32[8,1,2048]{2,1,0:T(1,128)} copy(f32[8,1,2048]{2,1,0:T(1,128)} %bitcast.1) | data formatting | bytes 131072
  97.2 1.7 %copy.10 = bf16[4,2,8,2048]{3,2,1,0:T(8,128)(2,1)} copy(bf16[4,2,8,2048]{3,2,1,0:T(8,128)(2,1)} %get-tuple-element.11) | data formatting | bytes 524288

commit v2 on v1

v2 whole, which is shorter than its diff:
```python
import functools
import math

import jax
import jax.numpy as jnp
from jax import lax
from jax.experimental import pallas as pl
from jax.experimental.pallas import tpu as pltpu
from jax.sharding import PartitionSpec as P

HANDOVERS = 8
PARTS = 4
VMEM_BYTES = 48 << 20
MESH = pl.DeviceIdType.MESH


def cuts(total, ends):
    edges = [0] + [e for e in ends if 0 < e < total] + [total]
    return list(zip(edges[:-1], edges[1:]))


def kernel(
    sections,
    owners,
    offsets_ref,
    assign_ref,
    fronts_hbm,
    extrap_ref,
    images_ref,
    last_ref,
    fronts_ref,
    oper,
    padded,
    outbox,
    inbox,
    half_image,
    slot_image,
    near_out,
    near_in,
    mate_out,
    mate_in,
    tail_out,
    tail_in,
    front_sem,
    load_sem,
    wave_send,
    wave_recv,
    near_send,
    near_recv,
    mate_send,
    mate_recv,
    tail_send,
    tail_recv,
):
    nfield, freqs, slots, _ = fronts_ref.shape
    nblk, band, block = extrap_ref.shape[1], extrap_ref.shape[2], extrap_ref.shape[-1]
    reach = band // 2
    half = owners // 2
    scale = 1.0 / math.sqrt(2.0 * freqs * owners)
    final = HANDOVERS - 1
    me = lax.axis_index("depth")
    depth = sections * owners
    section = me // owners
    owner = me % owners
    upper = owner // half
    lane = owner % half
    ahead = (me + owners) % depth
    behind = (me + depth - owners) % depth

    groups = cuts(nblk, (6, 12))
    parts = cuts(nblk, (6, 14))
    halves = cuts(nblk, (nblk // 2,))

    def front_load(freq):
        return pltpu.make_async_copy(
            fronts_hbm.at[:, freq], fronts_ref.at[:, freq], front_sem.at[freq]
        )

    def load(freq, part):
        lo, hi = groups[part]
        rows = pl.ds(lo, hi - lo)
        return pltpu.make_async_copy(
            extrap_ref.at[freq, rows], oper.at[freq, rows], load_sem.at[freq, part]
        )

    for freq in range(freqs):
        front_load(freq).start()
        for part in range(len(groups)):
            load(freq, part).start()

    def near(step):
        return section * owners + upper * half + (lane + step) % half

    def any_mate(step):
        return section * owners + (owner + step) % owners

    mate = section * owners + (owner + half) % owners
    barrier = pltpu.get_barrier_semaphore()
    greeted = [ahead] + ([behind] if sections > 2 else [])
    greeted = greeted + [any_mate(d) for d in range(1, owners)]
    for device in greeted:
        pl.semaphore_signal(barrier, inc=1, device_id={"depth": device}, device_id_type=MESH)

    offs = [offsets_ref[section, k] + reach for k in range(band)]
    slot_of = []
    for shot in range(slots):
        found = jnp.int32(0)
        for slot in range(slots):
            found = jnp.where(assign_ref[section, slot] == shot, slot, found)
        slot_of.append(found)

    def slot_for(target):
        chosen = slot_of[0]
        for shot in range(1, slots):
            chosen = jnp.where(target == shot, slot_of[shot], chosen)
        return chosen

    blank = jnp.zeros((reach,) + padded.shape[2:], padded.dtype)
    for freq in range(freqs):
        padded[freq, 0:reach] = blank
        padded[freq, reach + nblk : 2 * reach + nblk] = blank

    def unpack_front(freq):
        front_load(freq).wait()
        for b in range(nblk):
            cols = slice(b * block, (b + 1) * block)
            rows = [fronts_ref[c, freq, :, cols].astype(jnp.float32) for c in range(nfield)]
            padded[freq, reach + b] = jnp.concatenate(rows, axis=0).astype(padded.dtype)

    def remote(src, dst, send, recv, device):
        return pltpu.make_async_remote_copy(
            src_ref=src,
            dst_ref=dst,
            send_sem=send,
            recv_sem=recv,
            device_id={"depth": device},
            device_id_type=MESH,
        )

    def wave_copy(rnd, freq, part, lo, size):
        rows = pl.ds(lo, size)
        return remote(
            outbox.at[rnd, freq, rows],
            inbox.at[rnd, freq, rows],
            wave_send.at[rnd, freq, part],
            wave_recv.at[rnd, freq, part],
            ahead,
        )

    def near_copy(rnd, lo, size, device):
        rows = pl.ds(lo, size)
        return remote(
            near_out.at[rnd, rows],
            near_in.at[rnd, rows],
            near_send.at[rnd],
            near_recv.at[rnd],
            device,
        )

    def mate_copy(rnd):
        return remote(
            mate_out.at[rnd], mate_in.at[rnd], mate_send.at[rnd], mate_recv.at[rnd], mate
        )

    def tail_copy(piece, lo, size, device):
        rows = pl.ds(lo, size)
        return remote(
            tail_out.at[piece, rows],
            tail_in.at[piece, rows],
            tail_send.at[piece],
            tail_recv.at[piece],
            device,
        )

    def one_block(rnd, freq, b):
        lhs = jnp.concatenate([padded[freq, b + offs[k]] for k in range(band)], axis=1)
        rhs = jnp.concatenate(
            [
                jnp.concatenate([oper[freq, b, k, 0], oper[freq, b, k, 1]], axis=1)
                for k in range(band)
            ],
            axis=0,
        )
        both = jnp.dot(lhs, rhs, preferred_element_type=jnp.float32)
        re = [both[c * slots : (c + 1) * slots, :block] for c in range(nfield)]
        im = [both[c * slots : (c + 1) * slots, block:] for c in range(nfield)]
        new = [re[0] - im[1], im[0] + re[1], re[2] + im[3], re[3] - im[2]]
        rounded = jnp.concatenate(new, axis=0).astype(jnp.bfloat16)
        outbox[rnd, freq, b] = rounded
        wide = rounded.astype(jnp.float32)
        part = [wide[c * slots : (c + 1) * slots] for c in range(nfield)]
        image = part[0] * part[2] + part[1] * part[3]
        if freq > 0:
            image = image + half_image[b]
        if freq < freqs - 1:
            half_image[b] = image
        else:
            for slot in range(slots):
                slot_image[slot, pl.ds(b, 1), :] = image[slot : slot + 1] * scale

    def send_near(rnd):
        for step in range(half):
            column = (lane + step) % half
            near_out[rnd, step, 0] = slot_image[slot_for(upper * half + column)]
            near_out[rnd, step, 1] = slot_image[slot_for((1 - upper) * half + column)]
        for step in range(1, half):
            near_copy(rnd, step, 1, near(step)).start()

    def send_mate(rnd):
        near_copy(rnd, 1, half - 1, mate).wait_recv()
        mine = near_out[rnd, 0, 0]
        other = near_out[rnd, 0, 1]
        for step in range(1, half):
            mine = mine + near_in[rnd, step, 0]
            other = other + near_in[rnd, step, 1]
        images_ref[rnd] = mine
        mate_out[rnd] = other
        mate_copy(rnd).start()

    def finish_image(rnd):
        mate_copy(rnd).wait_recv()
        images_ref[rnd] = images_ref[rnd] + mate_in[rnd]

    def send_tail(piece):
        lo, hi = halves[piece]
        for step in range(owners):
            tail_out[piece, step] = slot_image[slot_for((owner + step) % owners), lo:hi]
        for step in range(1, owners):
            tail_copy(piece, step, 1, any_mate(step)).start()

    @pl.loop(0, HANDOVERS)
    def _(rnd):
        for freq in range(freqs):
            closing = freq == freqs - 1
            have = 0
            sent = 0
            imaged = 0
            for group, (lo, hi) in enumerate(groups):
                need = min(hi + reach, nblk)
                fresh = []
                while have < len(parts) and (parts[have][0] < need):
                    fresh.append(have)
                    have += 1

                @pl.when(rnd == 0)
                def _():
                    if group == 0:
                        unpack_front(freq)
                    load(freq, group).wait()

                @pl.when(rnd > 0)
                def _():
                    for part in fresh:
                        start, end = parts[part]
                        wave_copy(rnd - 1, freq, part, start, end - start).wait_recv()
                        padded[freq, reach + start : reach + end] = inbox[
                            rnd - 1, freq, start:end
                        ]

                for b in range(lo, hi):
                    one_block(rnd, freq, b)

                if freq == 0 and group == 0:

                    @pl.when(rnd == 0)
                    def _():
                        pl.semaphore_wait(barrier, len(greeted))

                outgoing = []
                while sent < len(parts) and parts[sent][1] <= hi:
                    outgoing.append(sent)
                    sent += 1

                @pl.when(rnd < final)
                def _():
                    for part in outgoing:
                        start, end = parts[part]
                        wave_copy(rnd, freq, part, start, end - start).start()

                @pl.when(rnd == final)
                def _():
                    nonlocal imaged
                    while closing and imaged < len(halves) and halves[imaged][1] <= hi:
                        send_tail(imaged)
                        imaged += 1
                    for b in range(lo, hi):
                        cols = slice(b * block, (b + 1) * block)
                        for c in range(nfield):
                            rows = slice(c * slots, (c + 1) * slots)
                            last_ref[c, freq, :, cols] = outbox[rnd, freq, b, rows, :]

            if freq == freqs - 2:

                @pl.when(rnd > 0)
                def _():
                    send_mate(rnd - 1)

        @pl.when(rnd < final)
        def _():
            send_near(rnd)

        @pl.when((rnd > 1) & (rnd < final))
        def _():
            finish_image(rnd - 2)

    @pl.loop(0, final)
    def _(rnd):
        for freq in range(freqs):
            for part, (lo, hi) in enumerate(parts):
                wave_copy(rnd, freq, part, lo, hi - lo).wait_send()
        near_copy(rnd, 1, half - 1, mate).wait_send()
        mate_copy(rnd).wait_send()

    finish_image(final - 2)
    finish_image(final - 1)
    for piece, (lo, hi) in enumerate(halves):
        tail_copy(piece, 1, owners - 1, mate).wait_recv()
        total = tail_out[piece, 0]
        for step in range(1, owners):
            total = total + tail_in[piece, step]
        images_ref[final, lo:hi] = total
    for piece in range(len(halves)):
        tail_copy(piece, 1, owners - 1, mate).wait_send()


def on_device(sections, owners, fronts, extrap, offsets, assign):
    nfield, freqs, slots, points = fronts.shape
    _, nblk, band, _, block, _ = extrap.shape
    moves = HANDOVERS - 1
    wave = (moves, freqs, nblk, nfield * slots, block)
    near = (moves, owners // 2, 2, nblk, block)
    mate = (moves, nblk, block)
    tail = (2, owners, nblk // 2, block)
    vmem = pl.BlockSpec(memory_space=pltpu.VMEM)
    smem = pl.BlockSpec(memory_space=pltpu.SMEM)
    hbm = pl.BlockSpec(memory_space=pltpu.HBM)
    dma = pltpu.SemaphoreType.DMA
    images, last = pl.pallas_call(
        functools.partial(kernel, sections, owners),
        out_shape=(
            jax.ShapeDtypeStruct((HANDOVERS, nblk, block), jnp.float32),
            jax.ShapeDtypeStruct(fronts.shape, fronts.dtype),
        ),
        in_specs=[smem, smem, hbm, hbm],
        out_specs=(vmem, vmem),
        scratch_shapes=[
            pltpu.VMEM(fronts.shape, fronts.dtype),
            pltpu.VMEM(extrap.shape, extrap.dtype),
            pltpu.VMEM((freqs, nblk + 2 * (band // 2), nfield * slots, block), fronts.dtype),
            pltpu.VMEM((HANDOVERS,) + wave[1:], fronts.dtype),
            pltpu.VMEM(wave, fronts.dtype),
            pltpu.VMEM((nblk, slots, block), jnp.float32),
            pltpu.VMEM((slots, nblk, block), jnp.float32),
            pltpu.VMEM(near, jnp.float32),
            pltpu.VMEM(near, jnp.float32),
            pltpu.VMEM(mate, jnp.float32),
            pltpu.VMEM(mate, jnp.float32),
            pltpu.VMEM(tail, jnp.float32),
            pltpu.VMEM(tail, jnp.float32),
            dma((freqs,)),
            dma((freqs, PARTS)),
            dma((moves, freqs, PARTS)),
            dma((moves, freqs, PARTS)),
            dma((moves,)),
            dma((moves,)),
            dma((moves,)),
            dma((moves,)),
            dma((2,)),
            dma((2,)),
        ],
        compiler_params=pltpu.CompilerParams(
            collective_id=0, has_side_effects=True, vmem_limit_bytes=VMEM_BYTES
        ),
    )(offsets, assign, fronts, extrap)
    return images.reshape(HANDOVERS, slots // owners, points), last


def solution(mesh):
    depth = mesh.shape["depth"]

    def program(fronts, extrap, offsets, assign):
        sections = offsets.shape[0]
        placed = (
            P(None, ("groups", "depth"), None, None),
            P("depth", None, None, None, None, None),
            P(),
            P(),
        )
        return jax.shard_map(
            functools.partial(on_device, sections, depth // sections),
            mesh=mesh,
            in_specs=placed,
            out_specs=(
                P(None, ("groups", "depth"), None),
                P(None, ("groups", "depth"), None, None),
            ),
            check_vma=False,
        )(fronts, extrap, offsets, assign)

    return program
```

time: 99.1 us -> 96.9 us (0.978)
  Pallas kernels: 95.1 us -> 92.4 us
    pallas_call x1, Pallas kernels: 95.1 us -> 92.4 us  [on_device(): pl.pallas_call(functools.partial(kernel, sections, owners), out_shape=(ja...]
    unnamed x2 -> x8, local copies, waits for them, and re-layouts: 3.14 us -> 3.63 us
where the time goes in v2:
time: 96.9 us; the launch traced here: 96.7 us
  Pallas kernels  92.4 us (95%)
  local copies, waits for them, and re-layouts  3.63 us (4%)
    pallas_call x1, Pallas kernels, on_device(): pl.pallas_call(functools.partial(kernel, sections, owners), out_shape=(ja...  92.4 us
    unnamed x8, local copies, waits for them, and re-layouts  3.63 us

profile of v2, /device:TPU:0, one launch (start us, length us, event | category | flops | bytes accessed | tf_op | source)
XLA Modules:
  0.0 96.7 jit_solution(6680994230854405759)
XLA Ops:
  0.6 0.0 copy-start
  0.6 0.9 copy-done
  1.6 0.0 copy-start.1
  1.6 0.7 copy-done.1
  2.3 0.0 copy-start.2
  2.3 0.7 copy-done.2
  2.9 92.4 %shard_map.59 = (f32[8,16,128]{2,1,0:T(8,128)S(1)}, bf16[4,2,8,2048]{3,2,1,0:T(8,128)(2,1)S(1)}) custom-call(s32[2,5]{1,0:T(2,128)S(1)} %copy-done.1, s32[2,8]{1,0:T(2,128)S(1)} %copy-done.2, bf16[4,2,8,2048]{3,2,1,0:T(8,128)(2,1)S(1)} %copy-done, bf16[2,16,5,2,128,128]{5,4,3,2,1,0:T(8,128)(2,1)} %extrap_ref.1), custom_call_target="tpu_custom_call" | custom-call | tf_op jit(solution)/shard_map/pallas_call | solution.py:338
  95.3 0.6 copy.9
  96.0 0.7 copy.10
Async XLA Ops:
  0.6 1.0 copy-start
  1.6 0.7 copy-start.1
  2.3 0.7 copy-start.2

commit v3 on v2

--- a/solution.py
+++ b/solution.py
@@ -67,8 +67,8 @@
     ahead = (me + owners) % depth
     behind = (me + depth - owners) % depth
 
-    groups = cuts(nblk, (6, 12))
-    parts = cuts(nblk, (6, 14))
+    groups = cuts(nblk, (2, 8, 12))
+    parts = cuts(nblk, (2, 8, 14))
     halves = cuts(nblk, (nblk // 2,))
 
     def front_load(freq):

time: 96.9 us -> 96.5 us (level)
  no operation moved by 1% of the time
where the time goes in v3:
time: 96.5 us; the launch traced here: 96.3 us
  Pallas kernels  92 us (95%)
  local copies, waits for them, and re-layouts  3.63 us (4%)
    pallas_call x1, Pallas kernels, on_device(): pl.pallas_call(functools.partial(kernel, sections, owners), out_shape=(ja...  92 us
    unnamed x8, local copies, waits for them, and re-layouts  3.63 us

profile of v3, /device:TPU:0, one launch (start us, length us, event | category | flops | bytes accessed | tf_op | source)
XLA Modules:
  0.0 96.3 jit_solution(4265124782929517481)
XLA Ops:
  0.6 0.0 copy-start
  0.6 0.9 copy-done
  1.6 0.0 copy-start.1
  1.6 0.7 copy-done.1
  2.3 0.0 copy-start.2
  2.3 0.7 copy-done.2
  2.9 92.0 %shard_map.59 = (f32[8,16,128]{2,1,0:T(8,128)S(1)}, bf16[4,2,8,2048]{3,2,1,0:T(8,128)(2,1)S(1)}) custom-call(s32[2,5]{1,0:T(2,128)S(1)} %copy-done.1, s32[2,8]{1,0:T(2,128)S(1)} %copy-done.2, bf16[4,2,8,2048]{3,2,1,0:T(8,128)(2,1)S(1)} %copy-done, bf16[2,16,5,2,128,128]{5,4,3,2,1,0:T(8,128)(2,1)} %extrap_ref.1), custom_call_target="tpu_custom_call" | custom-call | tf_op jit(solution)/shard_map/pallas_call | solution.py:338
  94.9 0.6 copy.9
  95.6 0.7 copy.10
Async XLA Ops:
  0.6 1.0 copy-start
  1.6 0.7 copy-start.1
  2.3 0.7 copy-start.2
